TPU v7x, 128 devices: a whole 4x4x4 slice. The times are simulated.
128 devices in a mesh: pb: 8 (over z_hi, x), ka: 16 (over z_lo, y, core).
Axes of the slice: x: 4, y: 4, z: 4 (z_hi: 2, z_lo: 2; z = z_hi * 2 + z_lo), core: 2. Of those that a mesh axis runs over, the one named last changes fastest.
Arguments:
- feat_first: bfloat16 [32768, 128], P(('pb', 'ka')), may hold values from -16 to 16
- feat_second: bfloat16 [32768, 128], P(('ka', 'pb')), may hold values from -18 to 18
- value_weight: bfloat16 [128, 128], replicated, may hold values from -0.5 to 0.5
- out_weight: bfloat16 [128, 128], replicated, may hold values from -0.5 to 0.5
- conv_weight: bfloat16 [3, 3, 128, 128], replicated, may hold values from -0.1875 to 0.1875
- conv_bias: bfloat16 [128], replicated, may hold values from -3 to 3
Outputs:
- refined: bfloat16 [128, 256, 128], P(('pb', 'ka'))
All inputs are finite; a program needn't handle non-finite values.
Results may differ from a plain program's by a relative error of at most 0.0055.
Values may be sent and summed in bfloat16 or wider, within the bound.
No kernel may reach another device: no remote copies, remote signals or barrier semaphores. Data moves between devices by JAX's collectives and lax.ppermute only.
A program may use at most 192 MiB of HBM per device.

v0:
```python
import jax
import jax.numpy as jnp
from jax import lax
from jax.sharding import PartitionSpec as P

WIMG = 256
floor_score = -1e30


def joined(value, axis, join):
    pieces = jax.tree.map(lambda part: lax.all_gather(part, axis), value)
    head = jax.tree.map(lambda part: part[0], pieces)
    tail = jax.tree.map(lambda part: part[1:], pieces)
    subtotal, _ = lax.scan(lambda subtotal, share: (join(subtotal, share), None), head, tail)
    return subtotal


def padded_2(block, sides, width):
    for axis, dim in sides:
        count = lax.axis_size(axis)
        forward = [(i, i + 1) for i in range(count - 1)]
        backward = [(target, source) for source, target in forward]
        low = lax.ppermute(
            lax.slice_in_dim(block, block.shape[dim] - width, None, axis=dim), axis, forward
        )
        high = lax.ppermute(lax.slice_in_dim(block, 0, width, axis=dim), axis, backward)
        block = jnp.concatenate([low, block, high], axis=dim)
    return block


def combine_parts(earlier, later):
    new_peak = jnp.maximum(earlier[0], later[0])
    early_factor = jnp.exp(earlier[0] - new_peak)
    late_factor = jnp.exp(later[0] - new_peak)
    new_mass = earlier[1] * early_factor + later[1] * late_factor
    new_weighted = earlier[2] * early_factor[:, None] + later[2] * late_factor[:, None]
    return (new_peak, new_mass, new_weighted)


def refine(padded, center, conv_weight, conv_bias):
    num_rows, num_cols, channels = center.shape
    accum_sum = jnp.zeros((num_rows * num_cols, channels), jnp.float32)
    for row_shift in range(3):
        for col_shift in range(3):
            window = padded[
                row_shift : row_shift + num_rows, col_shift : col_shift + num_cols
            ].reshape(num_rows * num_cols, channels)
            accum_sum = accum_sum + jnp.dot(
                window, conv_weight[row_shift, col_shift], preferred_element_type=jnp.float32
            )
    conv_out = accum_sum.reshape(num_rows, num_cols, channels) + conv_bias.astype(jnp.float32)
    return (center.astype(jnp.float32) + jax.nn.gelu(conv_out)).astype(jnp.bfloat16)


def local(feat_first, feat_second, value_weight, out_weight, conv_weight, conv_bias):
    own_rows, feat_width = feat_first.shape
    score_scale = feat_width ** (-0.5)
    values = jnp.dot(feat_second, value_weight, preferred_element_type=jnp.float32).astype(
        jnp.bfloat16
    )
    queries = lax.all_gather(feat_first, "ka", axis=0, tiled=True)
    total_rows = queries.shape[0]
    block_rows = min(1024, total_rows)
    num_blocks = total_rows // block_rows
    query_blocks = queries.reshape(num_blocks, block_rows, feat_width)
    start_carry = (
        jnp.full((num_blocks, block_rows), floor_score, jnp.float32),
        jnp.zeros((num_blocks, block_rows), jnp.float32),
        jnp.zeros((num_blocks, block_rows, feat_width), jnp.float32),
    )
    keys_part = lax.all_gather(feat_second, "pb", axis=0, tiled=True)
    values_part = lax.all_gather(values, "pb", axis=0, tiled=True)

    def update(members):
        query_block, old_peak, old_mass, old_weighted = members
        scores = (
            jnp.einsum("qc,kc->qk", query_block, keys_part, preferred_element_type=jnp.float32)
            * score_scale
        )
        new_peak = jnp.maximum(old_peak, jnp.max(scores, axis=1))
        expo = jnp.exp(scores - new_peak[:, None])
        decay_factor = jnp.exp(old_peak - new_peak)
        new_mass = old_mass * decay_factor + jnp.sum(expo, axis=1)
        new_weighted = old_weighted * decay_factor[:, None] + jnp.dot(
            expo.astype(jnp.bfloat16), values_part, preferred_element_type=jnp.float32
        )
        return (new_peak, new_mass, new_weighted)

    row_peak, row_mass, weighted = lax.map(update, (query_blocks,) + tuple(start_carry))
    row_peak = row_peak.reshape(total_rows)
    row_mass = row_mass.reshape(total_rows)
    weighted = weighted.reshape(total_rows, feat_width)
    own_start = lax.axis_index("ka") * own_rows
    merged = joined((row_peak, row_mass, weighted), "ka", combine_parts)
    mass_own = lax.dynamic_slice_in_dim(merged[1], own_start, own_rows, 0)
    weighted_own = lax.dynamic_slice_in_dim(merged[2], own_start, own_rows, 0)
    message = (weighted_own / mass_own[:, None]).astype(jnp.bfloat16)
    mixed_rows = (
        feat_first.astype(jnp.float32)
        + jnp.dot(message, out_weight, preferred_element_type=jnp.float32)
    ).astype(jnp.bfloat16)
    strip_rows = own_rows // WIMG
    strip_image = mixed_rows.reshape(strip_rows, WIMG, feat_width)
    tile_image = lax.all_to_all(strip_image, "ka", split_axis=1, concat_axis=0, tiled=True)
    padded = padded_2(tile_image, (("pb", 0), ("ka", 1)), 1)
    result = refine(padded, tile_image, conv_weight, conv_bias)
    refined = lax.all_to_all(result, "ka", split_axis=0, concat_axis=1, tiled=True)
    return refined


def solution(mesh):
    in_specs = (P(("pb", "ka"), None), P(("ka", "pb"), None), P(), P(), P(), P())
    out_specs = P(("pb", "ka"), None, None)
    return jax.shard_map(local, mesh=mesh, in_specs=in_specs, out_specs=out_specs, check_vma=False)
```

profile of v0, /device:TPU:7, one launch (start us, length us, event | category | flops | bytes accessed | tf_op | source)
XLA Modules:
  0.0 424.0 jit_solution(18136325351554592396)
XLA Ops:
  8.3 29.1 %all_gather.19 = bf16[2048,128]{1,0:T(8,128)(2,1)S(1)} all-gather(bf16[256,128]{1,0:T(8,128)(2,1)} %param.11), channel_id=1, replica_groups=mesh['pb'=8,'ka'=16] {'pb'}, dimensions={0}, use_global_device_ids=true | all-gather | bytes 589824 | tf_op jit(solution)/shard_map/all_gather | solution.py:71
  37.5 29.0 %all_gather.20 = bf16[2048,128]{1,0:T(8,128)(2,1)S(1)} all-gather(bf16[256,128]{1,0:T(8,128)(2,1)S(1)} %convolution_convert_fusion), channel_id=1, replica_groups=mesh['pb'=8,'ka'=16] {'pb'}, dimensions={0}, use_global_device_ids=true | all-gather | bytes 589824 | tf_op jit(solution)/shard_map/all_gather | solution.py:72
  66.5 28.9 %while.28 = (s32[]{:T(128)}, f32[4,1024]{1,0:T(4,128)S(1)}, f32[4,1024]{1,0:T(4,128)S(1)}, f32[4,1024,128]{2,1,0:T(8,128)}, bf16[4,1024,128]{2,1,0:T(8,128)(2,1)...) while((s32[]{:T(128)}, f32[4,1024]{1,0:T(4,128)S(1)}, ...), condition=%wide.region_3.4_spmd, body=%wide.region_0.3_spmd.sunk | while | flops 1090654208 | bytes 27063396 | solution.py:89
  76.0 2.8 fusion.80
  83.2 2.8 fusion.80
  90.4 2.8 fusion.80
  95.4 33.9 %all-gather = f32[16,1,4096]{2,1,0:T(1,128)S(1)} all-gather(f32[1,1,4096]{2,1,0:T(1,128)S(1)} %reshape.97), channel_id=1, replica_groups=mesh['pb'=8,'ka'=16] {'ka'}, dimensions={0}, use_global_device_ids=true | all-gather | bytes 278528 | tf_op jit(solution)/shard_map/all_gather | solution.py:11
  129.4 17.3 %all-gather.1 = f32[16,1,4096]{2,1,0:T(1,128)S(1)} all-gather(f32[1,1,4096]{2,1,0:T(1,128)S(1)} %reshape.99), channel_id=1, replica_groups=mesh['pb'=8,'ka'=16] {'ka'}, dimensions={0}, use_global_device_ids=true | all-gather | bytes 278528 | tf_op jit(solution)/shard_map/all_gather | solution.py:11
  147.1 135.8 %all-gather.7.cloned.1.call-done = f32[16,4096,128]{2,1,0:T(8,128)} async-done(((f32[1,4096,128]{2,1,0:T(8,128)}), f32[16,4096,128]{2,1,0:T(8,128)}) %all-gather.7.cloned.1.call-update) | async-done | bytes 33554448 | tf_op jit(solution)/shard_map/all_gather | solution.py:11
  282.9 21.8 %slice.127 = f32[15,4096,128]{2,1,0:T(8,128)} slice(f32[16,4096,128]{2,1,0:T(8,128)} %all-gather.7.cloned.1.call-done), slice={[1:16], [0:4096], [0:128]} | slice | bytes 62914560 | tf_op jit(solution)/shard_map/slice | solution.py:13
  306.4 63.9 %while.29 = (s32[]{:T(128)}, f32[4096]{0:T(1024)S(1)}, f32[4096]{0:T(1024)S(1)}, f32[4096,128]{1,0:T(8,128)S(1)}, f32[15,4096]{1,0:T(8,128)S(1)}, /*index=5*/f32...) while((s32[]{:T(128)}, f32[4096]{0:T(1024)S(1)}, f32[4096]{0:T(1024)S(1)}, f32[4096,128]{1,0:T(8,128)S(1)}, ...), condition=%wide.region_5.6_spmd, body=%wide.region_4.5_spmd.sunk | while | flops 1597442 | bytes 6520925 | solution.py:14
  306.5 4.2 fusion.81
  310.8 4.2 fusion.81
  315.0 4.2 fusion.81
  319.3 4.2 fusion.81
  323.6 4.2 fusion.81
  327.8 4.2 fusion.81
  332.1 4.2 fusion.81
  336.3 4.2 fusion.81
  340.6 4.2 fusion.81
  344.8 4.2 fusion.81
  349.1 4.2 fusion.81
  353.3 4.2 fusion.81
  357.6 4.2 fusion.81
  361.9 4.2 fusion.81
  366.1 4.2 fusion.81
  372.3 9.9 %all_to_all.24 = bf16[16,2,1024]{2,1,0:T(2,128)(2,1)S(1)} all-to-all(bf16[16,2,1024]{2,1,0:T(2,128)(2,1)S(1)} %reshape.109), channel_id=1, replica_groups=mesh['pb'=8,'ka'=16] {'ka'}, dimensions={0} | all-to-all | bytes 131072 | tf_op jit(solution)/shard_map/all_to_all | solution.py:104
  382.3 4.6 %collective-permute-start = (bf16[1,16,128]{2,1,0:T(8,128)(2,1)S(1)}, bf16[1,16,128]{2,1,0:T(8,128)(2,1)S(1)}, u32[]{:S(2)}, u32[]{:S(2)}) collective-permute-start(bf16[1,16,128]{2,1,0:T(8,128)(2,1)S(1)} %copy.19), channel_id=1, source_target_pairs={{0,16},{16,32},{32,48},{48,64},{64,80},{80,96},{96,112},{1,17},{17... | collective-permute-start | bytes 12296 | tf_op jit(solution)/shard_map/ppermute | solution.py:23
  388.9 6.0 %collective-permute-done.1 = bf16[1,16,128]{2,1,0:T(8,128)(2,1)S(1)} collective-permute-done((bf16[1,16,128]{2,1,0:T(8,128)(2,1)S(1)}, bf16[1,16,128]{2,1,0:T(8,128)(2,1)S(1)}, u32[]{:S(2)}, u32[]{:S(2)}) %collective-permute-start.1) | collective-permute-done | bytes 4128 | tf_op jit(solution)/shard_map/ppermute | solution.py:26
  394.9 3.9 collective-permute-start.2
  400.9 2.9 collective-permute-done.3
  405.2 11.3 %all_to_all.25 = bf16[16,16,128]{2,1,0:T(8,128)(2,1)S(1)} all-to-all(bf16[16,16,128]{2,1,0:T(8,128)(2,1)S(1)} %fusion.30), channel_id=1, replica_groups=mesh['pb'=8,'ka'=16] {'ka'}, dimensions={0} | all-to-all | bytes 131072 | tf_op jit(solution)/shard_map/all_to_all | solution.py:107
  (116 shorter events, 33.0 us)
Async XLA Ops:
  6.5 0.8 copy-start
  6.5 59.9 %all-gather.5.cloned.1.call-start = ((), (), s32[]{:S(2)}) async-start(), calls=%async_computation.2 | async-start | bytes 1114112 | tf_op jit(solution)/shard_map/all_gather | solution.py:61
  7.3 275.6 %all-gather.7.cloned.1.call-start = ((), (), s32[]{:S(2)}) async-start(), calls=%async_computation.3 | async-start | bytes 35651584 | tf_op jit(solution)/shard_map/all_gather | solution.py:11
  306.4 64.0 %copy-start.3 = (bf16[256,128]{1,0:T(8,128)(2,1)S(1)}, bf16[256,128]{1,0:T(8,128)(2,1)}, u32[]{:S(2)}) copy-start(bf16[256,128]{1,0:T(8,128)(2,1)} %param.10) | copy-start | bytes 196612
  306.4 64.0 %copy-start.4 = (bf16[128,128]{1,0:T(8,128)(2,1)S(1)}, bf16[128,128]{1,0:T(8,128)(2,1)}, u32[]{:S(2)}) copy-start(bf16[128,128]{1,0:T(8,128)(2,1)} %param.13) | copy-start | bytes 98308
  306.4 82.4 %copy-start.5 = (bf16[128]{0:T(256)(128)(2,1)S(1)}, bf16[128]{0:T(256)(128)(2,1)}, u32[]{:S(2)}) copy-start(bf16[128]{0:T(256)(128)(2,1)} %param.15) | copy-start | bytes 772
  306.4 94.3 %copy-start.2 = (bf16[3,3,128,128]{3,2,1,0:T(8,128)(2,1)S(1)}, bf16[3,3,128,128]{3,2,1,0:T(8,128)(2,1)}, u32[]{:S(2)}) copy-start(bf16[3,3,128,128]{3,2,1,0:T(8,128)(2,1)} %param.14) | copy-start | bytes 884740
  370.3 46.8 %copy-start.1 = (bf16[128,128]{1,0:T(8,128)(2,1)S(1)}, bf16[128,128]{1,0:T(8,128)(2,1)}, u32[]{:S(2)}) copy-start(bf16[128,128]{1,0:T(8,128)(2,1)} %param.12) | copy-start | bytes 98308
  382.3 6.6 %collective-permute-start = (bf16[1,16,128]{2,1,0:T(8,128)(2,1)S(1)}, bf16[1,16,128]{2,1,0:T(8,128)(2,1)S(1)}, u32[]{:S(2)}, u32[]{:S(2)}) collective-permute-start(bf16[1,16,128]{2,1,0:T(8,128)(2,1)S(1)} %copy.19), channel_id=1, source_target_pairs={{0,16},{16,32},{32,48},{48,64},{64,80},{80,96},{96,112},{1,17},{17... | collective-permute-start | bytes 12296 | tf_op jit(solution)/shard_map/ppermute | solution.py:23
  386.9 8.0 %collective-permute-start.1 = (bf16[1,16,128]{2,1,0:T(8,128)(2,1)S(1)}, bf16[1,16,128]{2,1,0:T(8,128)(2,1)S(1)}, u32[]{:S(2)}, u32[]{:S(2)}) collective-permute-start(bf16[1,16,128]{2,1,0:T(8,128)(2,1)S(1)} %copy.20), channel_id=1, source_target_pairs={{16,0},{32,16},{48,32},{64,48},{80,64},{96,80},{112,96},{17,1},{33... | collective-permute-start | bytes 12296 | tf_op jit(solution)/shard_map/ppermute | solution.py:26
  394.9 6.0 %collective-permute-start.2 = (bf16[18,1,128]{2,1,0:T(2,128)(2,1)S(1)}, bf16[18,1,128]{2,1,0:T(2,128)(2,1)S(1)}, u32[]{:S(2)}, u32[]{:S(2)}) collective-permute-start(bf16[18,1,128]{2,1,0:T(2,128)(2,1)S(1)} %get-tuple-element.135), channel_id=1, source_target_pairs={{0,1},{1,2},{2,3},{3,4},{4,5},{5,6},{6,7},{7,8},{8,9},{9,10},{10,1... | collective-permute-start | bytes 13832 | tf_op jit(solution)/shard_map/ppermute | solution.py:23
  398.8 5.0 %collective-permute-start.3 = (bf16[18,1,128]{2,1,0:T(2,128)(2,1)S(1)}, bf16[18,1,128]{2,1,0:T(2,128)(2,1)S(1)}, u32[]{:S(2)}, u32[]{:S(2)}) collective-permute-start(bf16[18,1,128]{2,1,0:T(2,128)(2,1)S(1)} %get-tuple-element.136), channel_id=1, source_target_pairs={{1,0},{2,1},{3,2},{4,3},{5,4},{6,5},{7,6},{8,7},{9,8},{10,9},{11,1... | collective-permute-start | bytes 13832 | tf_op jit(solution)/shard_map/ppermute | solution.py:26
Sparse Core Ops, SparseCore 0:
  9.0 35.1 all-gather.4
  95.5 187.3 all-gather.6
where the time goes:
time: 426 us; the launch traced here: 424 us
  waiting for transfers between devices  145 us (34%)
  blocking collectives  131 us (31%)
  other arithmetic  71.8 us (17%)
  local copies, waits for them, and re-layouts  26.5 us (6%)
  matrix products  23 us (5%)
  between operations  13.8 us (3%)
  starting transfers between devices  12.4 us (3%)
    all_gather x1, waiting for transfers between devices, joined(): pieces = jax.tree.map(lambda part: lax.all_gather(part, axis), value)  136 us
    add x15, other arithmetic, combine_parts(): earlier[2] * early_factor[:, None] + later[2] * late_factor[:, None]  62.5 us
    all_gather x2, blocking collectives, joined(): pieces = jax.tree.map(lambda part: lax.all_gather(part, axis), value)  51.2 us
    all_gather x1, blocking collectives, local(): keys_part = lax.all_gather(feat_second, 'pb', axis=0, tiled=True)  29.1 us
    all_gather x1, blocking collectives, local(): values_part = lax.all_gather(values, 'pb', axis=0, tiled=True)  29 us
    slice x3, local copies, waits for them, and re-layouts, joined(): tail = jax.tree.map(lambda part: part[1:], pieces)  21.8 us
    dot_general x4, matrix products, update(): jnp.dot(expo.astype(jnp.bfloat16), values_part, preferred_element_type=jn...  11.4 us
    all_to_all x1, blocking collectives, local(): lax.all_to_all(result, 'ka', split_axis=0, concat_axis=1, tiled=True)  11.3 us
  transfers between devices with their start and end apart: 6, of which 3 were waited for; matrix products, arithmetic and copies ran while one was open for 0% of the time, Pallas kernels for 0%

commit v1 on v0

--- a/solution.py
+++ b/solution.py
@@ -68,7 +68,9 @@
         jnp.zeros((num_blocks, block_rows), jnp.float32),
         jnp.zeros((num_blocks, block_rows, feat_width), jnp.float32),
     )
-    keys_part = lax.all_gather(feat_second, "pb", axis=0, tiled=True)
+    keys_part = jnp.concatenate(
+        lax.all_to_all(jnp.stack([feat_second] * lax.axis_size("pb")), "pb", 0, 0), axis=0
+    )
     values_part = lax.all_gather(values, "pb", axis=0, tiled=True)
 
     def update(members):

time: 426 us -> 399 us (0.937)
  blocking collectives: 131 us -> 96.1 us
  starting transfers between devices: 12.4 us -> 19.7 us
    all_gather x1 -> x0, blocking collectives: 29.1 us -> none  [local(): keys_part = lax.all_gather(feat_second, 'pb', axis=0, tiled=True)]
    all_to_all x0 -> x1, starting transfers between devices: none -> 7.53 us  [local(): lax.all_to_all(jnp.stack([feat_second] * lax.axis_size('pb')), 'pb', 0, 0)]
    all_gather x2, blocking collectives: 51.2 us -> 45.5 us  [joined(): pieces = jax.tree.map(lambda part: lax.all_gather(part, axis), value)]
  transfers between devices with their start and end apart: 6 -> 7, of which waited for: 3 -> 3; matrix products, arithmetic and copies ran while one was open for 0% -> 1% of each run, Pallas kernels for 0% -> 0%
where the time goes in v1:
time: 399 us; the launch traced here: 398 us
  waiting for transfers between devices  144 us (36%)
  blocking collectives  96.1 us (24%)
  other arithmetic  71.8 us (18%)
  local copies, waits for them, and re-layouts  28.2 us (7%)
  matrix products  23 us (6%)
  starting transfers between devices  19.7 us (5%)
  between operations  13.7 us (3%)
    all_gather x1, waiting for transfers between devices, joined(): pieces = jax.tree.map(lambda part: lax.all_gather(part, axis), value)  135 us
    add x15, other arithmetic, combine_parts(): earlier[2] * early_factor[:, None] + later[2] * late_factor[:, None]  62.5 us
    all_gather x2, blocking collectives, joined(): pieces = jax.tree.map(lambda part: lax.all_gather(part, axis), value)  45.5 us
    all_gather x1, blocking collectives, local(): values_part = lax.all_gather(values, 'pb', axis=0, tiled=True)  29.5 us
    slice x3, local copies, waits for them, and re-layouts, joined(): tail = jax.tree.map(lambda part: part[1:], pieces)  21.8 us
    dot_general x4, matrix products, update(): jnp.dot(expo.astype(jnp.bfloat16), values_part, preferred_element_type=jn...  11.4 us
    all_to_all x1, blocking collectives, local(): lax.all_to_all(result, 'ka', split_axis=0, concat_axis=1, tiled=True)  11.3 us
    all_to_all x1, blocking collectives, local(): lax.all_to_all(strip_image, 'ka', split_axis=1, concat_axis=0, tiled=True)  9.75 us
  transfers between devices with their start and end apart: 7, of which 3 were waited for; matrix products, arithmetic and copies ran while one was open for 1% of the time, Pallas kernels for 0%

profile of v1, /device:TPU:7, one launch (start us, length us, event | category | flops | bytes accessed | tf_op | source)
XLA Modules:
  0.0 397.6 jit_solution(228262811801622939)
XLA Ops:
  9.0 7.5 %all-to-all-start = ((bf16[8,256,128]{2,1,0:T(8,128)(2,1)}), bf16[8,256,128]{2,1,0:T(8,128)(2,1)S(1)}, u32[]{:S(2)}, u32[]{:S(2)}) async-start(bf16[8,256,128]{2,1,0:T(8,128)(2,1)} %stack.2), calls=%async_computation | async-start | bytes 1048576 | tf_op jit(solution)/shard_map/all_to_all | solution.py:72
  17.5 29.5 %all_gather.16 = bf16[2048,128]{1,0:T(8,128)(2,1)S(1)} all-gather(bf16[256,128]{1,0:T(8,128)(2,1)S(1)} %convolution_convert_fusion), channel_id=1, replica_groups=mesh['pb'=8,'ka'=16] {'pb'}, dimensions={0}, use_global_device_ids=true | all-gather | bytes 589824 | tf_op jit(solution)/shard_map/all_gather | solution.py:74
  47.1 28.9 %while.28 = (s32[]{:T(128)}, f32[4,1024]{1,0:T(4,128)S(1)}, f32[4,1024]{1,0:T(4,128)S(1)}, f32[4,1024,128]{2,1,0:T(8,128)}, bf16[4,1024,128]{2,1,0:T(8,128)(2,1)...) while((s32[]{:T(128)}, f32[4,1024]{1,0:T(4,128)S(1)}, ...), condition=%wide.region_3.4_spmd, body=%wide.region_0.3_spmd.sunk | while | flops 1090654208 | bytes 27063396 | solution.py:91
  49.3 2.8 fusion.80
  56.6 2.8 fusion.80
  71.1 2.8 fusion.80
  76.1 28.2 %all-gather.1 = f32[16,1,4096]{2,1,0:T(1,128)S(1)} all-gather(f32[1,1,4096]{2,1,0:T(1,128)S(1)} %reshape.105), channel_id=1, replica_groups=mesh['pb'=8,'ka'=16] {'ka'}, dimensions={0}, use_global_device_ids=true | all-gather | bytes 278528 | tf_op jit(solution)/shard_map/all_gather | solution.py:11
  104.3 17.3 %all-gather = f32[16,1,4096]{2,1,0:T(1,128)S(1)} all-gather(f32[1,1,4096]{2,1,0:T(1,128)S(1)} %reshape.103), channel_id=1, replica_groups=mesh['pb'=8,'ka'=16] {'ka'}, dimensions={0}, use_global_device_ids=true | all-gather | bytes 278528 | tf_op jit(solution)/shard_map/all_gather | solution.py:11
  122.0 134.8 %all-gather.7.cloned.1.call-done = f32[16,4096,128]{2,1,0:T(8,128)} async-done(((f32[1,4096,128]{2,1,0:T(8,128)}), f32[16,4096,128]{2,1,0:T(8,128)}) %all-gather.7.cloned.1.call-update) | async-done | bytes 33554448 | tf_op jit(solution)/shard_map/all_gather | solution.py:11
  256.8 21.8 %slice.127 = f32[15,4096,128]{2,1,0:T(8,128)} slice(f32[16,4096,128]{2,1,0:T(8,128)} %all-gather.7.cloned.1.call-done), slice={[1:16], [0:4096], [0:128]} | slice | bytes 62914560 | tf_op jit(solution)/shard_map/slice | solution.py:13
  280.4 63.9 %while.29 = (s32[]{:T(128)}, f32[4096]{0:T(1024)S(1)}, f32[4096]{0:T(1024)S(1)}, f32[4096,128]{1,0:T(8,128)S(1)}, f32[15,4096]{1,0:T(8,128)S(1)}, /*index=5*/f32...) while((s32[]{:T(128)}, f32[4096]{0:T(1024)S(1)}, f32[4096]{0:T(1024)S(1)}, f32[4096,128]{1,0:T(8,128)S(1)}, ...), condition=%wide.region_5.6_spmd, body=%wide.region_4.5_spmd.sunk | while | flops 1597442 | bytes 6520925 | solution.py:14
  280.5 4.2 %fusion.81 = f32[4096,128]{1,0:T(8,128)S(1)} fusion(f32[15,4096,128]{2,1,0:T(8,128)} %get-tuple-element.297, s32[]{:T(128)} %get-tuple-element.283, f32[4096,128]{1,0:T(8,128)S(1)} %get-tuple-element.286, f32[4096]{0:T(1024)S(1)} %get-tuple-element.246, f32[4096]{0:T(1024)S(1)} %get-tuple-element.247), kind=kLoop, calls=%fused_computation.17.clone.1 | loop fusion | flops 1572864 | bytes 6324228 | tf_op jit(solution)/shard_map/while/body/eval_jaxpr/add | solution.py:36
  284.7 4.2 %fusion.81 = f32[4096,128]{1,0:T(8,128)S(1)} fusion(f32[15,4096,128]{2,1,0:T(8,128)} %get-tuple-element.297, s32[]{:T(128)} %get-tuple-element.283, f32[4096,128]{1,0:T(8,128)S(1)} %get-tuple-element.286, f32[4096]{0:T(1024)S(1)} %get-tuple-element.246, f32[4096]{0:T(1024)S(1)} %get-tuple-element.247), kind=kLoop, calls=%fused_computation.17.clone.1 | loop fusion | flops 1572864 | bytes 6324228 | tf_op jit(solution)/shard_map/while/body/eval_jaxpr/add | solution.py:36
  289.0 4.2 %fusion.81 = f32[4096,128]{1,0:T(8,128)S(1)} fusion(f32[15,4096,128]{2,1,0:T(8,128)} %get-tuple-element.297, s32[]{:T(128)} %get-tuple-element.283, f32[4096,128]{1,0:T(8,128)S(1)} %get-tuple-element.286, f32[4096]{0:T(1024)S(1)} %get-tuple-element.246, f32[4096]{0:T(1024)S(1)} %get-tuple-element.247), kind=kLoop, calls=%fused_computation.17.clone.1 | loop fusion | flops 1572864 | bytes 6324228 | tf_op jit(solution)/shard_map/while/body/eval_jaxpr/add | solution.py:36
  293.3 4.2 %fusion.81 = f32[4096,128]{1,0:T(8,128)S(1)} fusion(f32[15,4096,128]{2,1,0:T(8,128)} %get-tuple-element.297, s32[]{:T(128)} %get-tuple-element.283, f32[4096,128]{1,0:T(8,128)S(1)} %get-tuple-element.286, f32[4096]{0:T(1024)S(1)} %get-tuple-element.246, f32[4096]{0:T(1024)S(1)} %get-tuple-element.247), kind=kLoop, calls=%fused_computation.17.clone.1 | loop fusion | flops 1572864 | bytes 6324228 | tf_op jit(solution)/shard_map/while/body/eval_jaxpr/add | solution.py:36
  297.5 4.2 %fusion.81 = f32[4096,128]{1,0:T(8,128)S(1)} fusion(f32[15,4096,128]{2,1,0:T(8,128)} %get-tuple-element.297, s32[]{:T(128)} %get-tuple-element.283, f32[4096,128]{1,0:T(8,128)S(1)} %get-tuple-element.286, f32[4096]{0:T(1024)S(1)} %get-tuple-element.246, f32[4096]{0:T(1024)S(1)} %get-tuple-element.247), kind=kLoop, calls=%fused_computation.17.clone.1 | loop fusion | flops 1572864 | bytes 6324228 | tf_op jit(solution)/shard_map/while/body/eval_jaxpr/add | solution.py:36
  301.8 4.2 %fusion.81 = f32[4096,128]{1,0:T(8,128)S(1)} fusion(f32[15,4096,128]{2,1,0:T(8,128)} %get-tuple-element.297, s32[]{:T(128)} %get-tuple-element.283, f32[4096,128]{1,0:T(8,128)S(1)} %get-tuple-element.286, f32[4096]{0:T(1024)S(1)} %get-tuple-element.246, f32[4096]{0:T(1024)S(1)} %get-tuple-element.247), kind=kLoop, calls=%fused_computation.17.clone.1 | loop fusion | flops 1572864 | bytes 6324228 | tf_op jit(solution)/shard_map/while/body/eval_jaxpr/add | solution.py:36
  306.0 4.2 %fusion.81 = f32[4096,128]{1,0:T(8,128)S(1)} fusion(f32[15,4096,128]{2,1,0:T(8,128)} %get-tuple-element.297, s32[]{:T(128)} %get-tuple-element.283, f32[4096,128]{1,0:T(8,128)S(1)} %get-tuple-element.286, f32[4096]{0:T(1024)S(1)} %get-tuple-element.246, f32[4096]{0:T(1024)S(1)} %get-tuple-element.247), kind=kLoop, calls=%fused_computation.17.clone.1 | loop fusion | flops 1572864 | bytes 6324228 | tf_op jit(solution)/shard_map/while/body/eval_jaxpr/add | solution.py:36
  310.3 4.2 %fusion.81 = f32[4096,128]{1,0:T(8,128)S(1)} fusion(f32[15,4096,128]{2,1,0:T(8,128)} %get-tuple-element.297, s32[]{:T(128)} %get-tuple-element.283, f32[4096,128]{1,0:T(8,128)S(1)} %get-tuple-element.286, f32[4096]{0:T(1024)S(1)} %get-tuple-element.246, f32[4096]{0:T(1024)S(1)} %get-tuple-element.247), kind=kLoop, calls=%fused_computation.17.clone.1 | loop fusion | flops 1572864 | bytes 6324228 | tf_op jit(solution)/shard_map/while/body/eval_jaxpr/add | solution.py:36
  314.5 4.2 %fusion.81 = f32[4096,128]{1,0:T(8,128)S(1)} fusion(f32[15,4096,128]{2,1,0:T(8,128)} %get-tuple-element.297, s32[]{:T(128)} %get-tuple-element.283, f32[4096,128]{1,0:T(8,128)S(1)} %get-tuple-element.286, f32[4096]{0:T(1024)S(1)} %get-tuple-element.246, f32[4096]{0:T(1024)S(1)} %get-tuple-element.247), kind=kLoop, calls=%fused_computation.17.clone.1 | loop fusion | flops 1572864 | bytes 6324228 | tf_op jit(solution)/shard_map/while/body/eval_jaxpr/add | solution.py:36
  318.8 4.2 %fusion.81 = f32[4096,128]{1,0:T(8,128)S(1)} fusion(f32[15,4096,128]{2,1,0:T(8,128)} %get-tuple-element.297, s32[]{:T(128)} %get-tuple-element.283, f32[4096,128]{1,0:T(8,128)S(1)} %get-tuple-element.286, f32[4096]{0:T(1024)S(1)} %get-tuple-element.246, f32[4096]{0:T(1024)S(1)} %get-tuple-element.247), kind=kLoop, calls=%fused_computation.17.clone.1 | loop fusion | flops 1572864 | bytes 6324228 | tf_op jit(solution)/shard_map/while/body/eval_jaxpr/add | solution.py:36
  323.0 4.2 %fusion.81 = f32[4096,128]{1,0:T(8,128)S(1)} fusion(f32[15,4096,128]{2,1,0:T(8,128)} %get-tuple-element.297, s32[]{:T(128)} %get-tuple-element.283, f32[4096,128]{1,0:T(8,128)S(1)} %get-tuple-element.286, f32[4096]{0:T(1024)S(1)} %get-tuple-element.246, f32[4096]{0:T(1024)S(1)} %get-tuple-element.247), kind=kLoop, calls=%fused_computation.17.clone.1 | loop fusion | flops 1572864 | bytes 6324228 | tf_op jit(solution)/shard_map/while/body/eval_jaxpr/add | solution.py:36
  327.3 4.2 %fusion.81 = f32[4096,128]{1,0:T(8,128)S(1)} fusion(f32[15,4096,128]{2,1,0:T(8,128)} %get-tuple-element.297, s32[]{:T(128)} %get-tuple-element.283, f32[4096,128]{1,0:T(8,128)S(1)} %get-tuple-element.286, f32[4096]{0:T(1024)S(1)} %get-tuple-element.246, f32[4096]{0:T(1024)S(1)} %get-tuple-element.247), kind=kLoop, calls=%fused_computation.17.clone.1 | loop fusion | flops 1572864 | bytes 6324228 | tf_op jit(solution)/shard_map/while/body/eval_jaxpr/add | solution.py:36
  331.6 4.2 %fusion.81 = f32[4096,128]{1,0:T(8,128)S(1)} fusion(f32[15,4096,128]{2,1,0:T(8,128)} %get-tuple-element.297, s32[]{:T(128)} %get-tuple-element.283, f32[4096,128]{1,0:T(8,128)S(1)} %get-tuple-element.286, f32[4096]{0:T(1024)S(1)} %get-tuple-element.246, f32[4096]{0:T(1024)S(1)} %get-tuple-element.247), kind=kLoop, calls=%fused_computation.17.clone.1 | loop fusion | flops 1572864 | bytes 6324228 | tf_op jit(solution)/shard_map/while/body/eval_jaxpr/add | solution.py:36
  335.8 4.2 %fusion.81 = f32[4096,128]{1,0:T(8,128)S(1)} fusion(f32[15,4096,128]{2,1,0:T(8,128)} %get-tuple-element.297, s32[]{:T(128)} %get-tuple-element.283, f32[4096,128]{1,0:T(8,128)S(1)} %get-tuple-element.286, f32[4096]{0:T(1024)S(1)} %get-tuple-element.246, f32[4096]{0:T(1024)S(1)} %get-tuple-element.247), kind=kLoop, calls=%fused_computation.17.clone.1 | loop fusion | flops 1572864 | bytes 6324228 | tf_op jit(solution)/shard_map/while/body/eval_jaxpr/add | solution.py:36
  340.1 4.2 %fusion.81 = f32[4096,128]{1,0:T(8,128)S(1)} fusion(f32[15,4096,128]{2,1,0:T(8,128)} %get-tuple-element.297, s32[]{:T(128)} %get-tuple-element.283, f32[4096,128]{1,0:T(8,128)S(1)} %get-tuple-element.286, f32[4096]{0:T(1024)S(1)} %get-tuple-element.246, f32[4096]{0:T(1024)S(1)} %get-tuple-element.247), kind=kLoop, calls=%fused_computation.17.clone.1 | loop fusion | flops 1572864 | bytes 6324228 | tf_op jit(solution)/shard_map/while/body/eval_jaxpr/add | solution.py:36
  346.2 9.8 %all_to_all.29 = bf16[16,2,1024]{2,1,0:T(2,128)(2,1)S(1)} all-to-all(bf16[16,2,1024]{2,1,0:T(2,128)(2,1)S(1)} %reshape.115), channel_id=1, replica_groups=mesh['pb'=8,'ka'=16] {'ka'}, dimensions={0} | all-to-all | bytes 131072 | tf_op jit(solution)/shard_map/all_to_all | solution.py:106
  356.1 4.5 %collective-permute-start = (bf16[1,16,128]{2,1,0:T(8,128)(2,1)S(1)}, bf16[1,16,128]{2,1,0:T(8,128)(2,1)S(1)}, u32[]{:S(2)}, u32[]{:S(2)}) collective-permute-start(bf16[1,16,128]{2,1,0:T(8,128)(2,1)S(1)} %copy.19), channel_id=1, source_target_pairs={{0,16},{16,32},{32,48},{48,64},{64,80},{80,96},{96,112},{1,17},{17... | collective-permute-start | bytes 12296 | tf_op jit(solution)/shard_map/ppermute | solution.py:23
  362.6 6.0 %collective-permute-done.1 = bf16[1,16,128]{2,1,0:T(8,128)(2,1)S(1)} collective-permute-done((bf16[1,16,128]{2,1,0:T(8,128)(2,1)S(1)}, bf16[1,16,128]{2,1,0:T(8,128)(2,1)S(1)}, u32[]{:S(2)}, u32[]{:S(2)}) %collective-permute-start.1) | collective-permute-done | bytes 4128 | tf_op jit(solution)/shard_map/ppermute | solution.py:26
  368.6 3.9 collective-permute-start.2
  374.6 2.9 collective-permute-done.3
  378.9 11.3 %all_to_all.30 = bf16[16,16,128]{2,1,0:T(8,128)(2,1)S(1)} all-to-all(bf16[16,16,128]{2,1,0:T(8,128)(2,1)S(1)} %fusion.30), channel_id=1, replica_groups=mesh['pb'=8,'ka'=16] {'ka'}, dimensions={0} | all-to-all | bytes 131072 | tf_op jit(solution)/shard_map/all_to_all | solution.py:109
  (118 shorter events, 34.7 us)
Async XLA Ops:
  6.5 10.0 %copy-start = (bf16[128,128]{1,0:T(8,128)(2,1)S(1)}, bf16[128,128]{1,0:T(8,128)(2,1)}, u32[]{:S(2)}) copy-start(bf16[128,128]{1,0:T(8,128)(2,1)} %param.12) | copy-start | bytes 98308
  6.5 40.5 %all-gather.5.cloned.1.call-start = ((), (), s32[]{:S(2)}) async-start(), calls=%async_computation.3 | async-start | bytes 1114112 | tf_op jit(solution)/shard_map/all_gather | solution.py:61
  9.0 38.1 %all-to-all-start = ((bf16[8,256,128]{2,1,0:T(8,128)(2,1)}), bf16[8,256,128]{2,1,0:T(8,128)(2,1)S(1)}, u32[]{:S(2)}, u32[]{:S(2)}) async-start(bf16[8,256,128]{2,1,0:T(8,128)(2,1)} %stack.2), calls=%async_computation | async-start | bytes 1048576 | tf_op jit(solution)/shard_map/all_to_all | solution.py:72
  16.5 240.3 %all-gather.7.cloned.1.call-start = ((), (), s32[]{:S(2)}) async-start(), calls=%async_computation.4 | async-start | bytes 35651584 | tf_op jit(solution)/shard_map/all_gather | solution.py:11
  280.3 64.0 %copy-start.3 = (bf16[256,128]{1,0:T(8,128)(2,1)S(1)}, bf16[256,128]{1,0:T(8,128)(2,1)}, u32[]{:S(2)}) copy-start(bf16[256,128]{1,0:T(8,128)(2,1)} %param.10) | copy-start | bytes 196612
  280.3 64.0 %copy-start.4 = (bf16[128,128]{1,0:T(8,128)(2,1)S(1)}, bf16[128,128]{1,0:T(8,128)(2,1)}, u32[]{:S(2)}) copy-start(bf16[128,128]{1,0:T(8,128)(2,1)} %param.13) | copy-start | bytes 98308
  280.4 82.2 %copy-start.5 = (bf16[128]{0:T(256)(128)(2,1)S(1)}, bf16[128]{0:T(256)(128)(2,1)}, u32[]{:S(2)}) copy-start(bf16[128]{0:T(256)(128)(2,1)} %param.15) | copy-start | bytes 772
  280.4 94.1 %copy-start.2 = (bf16[3,3,128,128]{3,2,1,0:T(8,128)(2,1)S(1)}, bf16[3,3,128,128]{3,2,1,0:T(8,128)(2,1)}, u32[]{:S(2)}) copy-start(bf16[3,3,128,128]{3,2,1,0:T(8,128)(2,1)} %param.14) | copy-start | bytes 884740
  344.2 46.5 %copy-start.1 = (bf16[128,128]{1,0:T(8,128)(2,1)S(1)}, bf16[128,128]{1,0:T(8,128)(2,1)}, u32[]{:S(2)}) copy-start(bf16[128,128]{1,0:T(8,128)(2,1)} %param.12) | copy-start | bytes 98308
  356.1 6.5 %collective-permute-start = (bf16[1,16,128]{2,1,0:T(8,128)(2,1)S(1)}, bf16[1,16,128]{2,1,0:T(8,128)(2,1)S(1)}, u32[]{:S(2)}, u32[]{:S(2)}) collective-permute-start(bf16[1,16,128]{2,1,0:T(8,128)(2,1)S(1)} %copy.19), channel_id=1, source_target_pairs={{0,16},{16,32},{32,48},{48,64},{64,80},{80,96},{96,112},{1,17},{17... | collective-permute-start | bytes 12296 | tf_op jit(solution)/shard_map/ppermute | solution.py:23
  360.6 8.0 %collective-permute-start.1 = (bf16[1,16,128]{2,1,0:T(8,128)(2,1)S(1)}, bf16[1,16,128]{2,1,0:T(8,128)(2,1)S(1)}, u32[]{:S(2)}, u32[]{:S(2)}) collective-permute-start(bf16[1,16,128]{2,1,0:T(8,128)(2,1)S(1)} %copy.20), channel_id=1, source_target_pairs={{16,0},{32,16},{48,32},{64,48},{80,64},{96,80},{112,96},{17,1},{33... | collective-permute-start | bytes 12296 | tf_op jit(solution)/shard_map/ppermute | solution.py:26
  368.6 6.0 %collective-permute-start.2 = (bf16[18,1,128]{2,1,0:T(2,128)(2,1)S(1)}, bf16[18,1,128]{2,1,0:T(2,128)(2,1)S(1)}, u32[]{:S(2)}, u32[]{:S(2)}) collective-permute-start(bf16[18,1,128]{2,1,0:T(2,128)(2,1)S(1)} %get-tuple-element.135), channel_id=1, source_target_pairs={{0,1},{1,2},{2,3},{3,4},{4,5},{5,6},{6,7},{7,8},{8,9},{9,10},{10,1... | collective-permute-start | bytes 13832 | tf_op jit(solution)/shard_map/ppermute | solution.py:23
  372.5 5.0 %collective-permute-start.3 = (bf16[18,1,128]{2,1,0:T(2,128)(2,1)S(1)}, bf16[18,1,128]{2,1,0:T(2,128)(2,1)S(1)}, u32[]{:S(2)}, u32[]{:S(2)}) collective-permute-start(bf16[18,1,128]{2,1,0:T(2,128)(2,1)S(1)} %get-tuple-element.136), channel_id=1, source_target_pairs={{1,0},{2,1},{3,2},{4,3},{5,4},{6,5},{7,6},{8,7},{9,8},{10,9},{11,1... | collective-permute-start | bytes 13832 | tf_op jit(solution)/shard_map/ppermute | solution.py:26
Sparse Core Ops, SparseCore 0:
  9.0 35.2 all-gather.4
  76.1 180.6 all-gather.6
